TPU v7x, 256 devices: a whole 4x4x8 slice. The times are simulated.
256 devices in a mesh: dp: 32 (over y_lo, z, core), ctx: 8 (over y_hi, x).
Axes of the slice: x: 4, y: 4 (y_hi: 2, y_lo: 2; y = y_hi * 2 + y_lo), z: 8, core: 2. Of those that a mesh axis runs over, the one named last changes fastest.
Arguments:
- query_proj: bfloat16 [64, 512, 4096], P('dp', 'ctx'), may hold values from -5 to 5
- key_proj: bfloat16 [64, 512, 1024], P('dp', 'ctx'), may hold values from -5 to 5
- value_proj: bfloat16 [64, 512, 1024], P('dp', 'ctx'), may hold values from -6 to 6
- grad_attn: bfloat16 [64, 512, 4096], P('dp', 'ctx'), may hold values from -6 to 6
- doc_lengths: int32 [64, 8], replicated, may hold values from 1 to 128, 512 in all within a row
- mask_tiles: int32 [64, 8, 8], replicated, may hold values from 0 to 1, as said below
- pair_flags: int32 [32], replicated, may hold values from 0 to 1, as said below
Outputs:
- attn_out: bfloat16 [64, 512, 4096], P('dp', 'ctx')
- grad_query: bfloat16 [64, 512, 4096], P('dp', 'ctx')
- grad_key: bfloat16 [64, 512, 1024], P('dp', 'ctx')
- grad_value: bfloat16 [64, 512, 1024], P('dp', 'ctx')
Inputs may be any that keep to these rules, and one draw needn't show every extreme that they name: `doc_lengths`: each row sums to 512. mask_tiles[n, t, t] = 1 for every sequence n and tile t. pair_flags[r] = pair_flags[r XOR (16)] for every r.
All inputs are finite; a program needn't handle non-finite values.
Results may differ from a plain program's by a relative error of at most 0.03.
Values may be sent and summed in bfloat16 or wider, within the bound.
A program may use at most 128 MiB of HBM per device.

v0:
```python
import jax
import jax.numpy as jnp
from jax import lax
from jax.sharding import PartitionSpec as P

QUERY_HEADS = 32
KEY_VALUE_HEADS = 8
HEAD_SIZE = 128


def from_partner(value, axis, distance):
    mask = 2**distance
    pairs = [(source, source ^ mask) for source in range(lax.axis_size(axis))]
    return lax.ppermute(value, axis, pairs)


def sequence_core(
    query_rows, sequence_keys, sequence_values, sequence_gradients, lengths, tile_table, row_start
):
    rows = query_rows.shape[0]
    length_total = sequence_keys.shape[0]
    groups = sequence_keys.shape[1] // HEAD_SIZE
    group_ratio = QUERY_HEADS // KEY_VALUE_HEADS
    scale = HEAD_SIZE ** (-0.5)
    row_pos = row_start + jnp.arange(rows, dtype=jnp.int32)
    col_pos = jnp.arange(length_total, dtype=jnp.int32)
    ends = jnp.cumsum(lengths)[:-1]
    row_doc = jnp.sum((row_pos[:, None] >= ends[None, :]).astype(jnp.int32), axis=1)
    col_doc = jnp.sum((col_pos[:, None] >= ends[None, :]).astype(jnp.int32), axis=1)
    tile_count = tile_table.shape[0]
    tile_len = length_total // tile_count
    tile_ids = jnp.arange(tile_count, dtype=jnp.int32)
    row_pick = ((row_pos // tile_len)[:, None] == tile_ids[None, :]).astype(jnp.float32)
    col_pick = ((col_pos // tile_len)[:, None] == tile_ids[None, :]).astype(jnp.float32)
    tile_map = jnp.dot(jnp.dot(row_pick, tile_table.astype(jnp.float32)), col_pick.T) > 0.5
    allowed = (
        (col_pos[None, :] <= row_pos[:, None])
        & ((col_doc[None, :] == row_doc[:, None]) | (col_doc[None, :] == 0))
        & tile_map
    )
    heads_of_queries = query_rows.reshape(rows, groups, group_ratio, HEAD_SIZE)
    heads_of_keys = sequence_keys.reshape(length_total, groups, HEAD_SIZE)
    heads_of_values = sequence_values.reshape(length_total, groups, HEAD_SIZE)
    head_gradients = sequence_gradients.reshape(rows, groups, group_ratio, HEAD_SIZE)
    scores = (
        jnp.einsum(
            "igrd,jgd->grij", heads_of_queries, heads_of_keys, preferred_element_type=jnp.float32
        )
        * scale
    )
    scores = jnp.where(allowed, scores, -1e30)
    peak = jnp.max(scores, axis=-1, keepdims=True)
    expd = jnp.where(allowed, jnp.exp(scores - peak), 0.0)
    probs = expd / jnp.sum(expd, axis=-1, keepdims=True)
    probs_b = probs.astype(jnp.bfloat16)
    attn = jnp.einsum(
        "grij,jgd->igrd", probs_b, heads_of_values, preferred_element_type=jnp.float32
    ).astype(jnp.bfloat16)
    delta = jnp.transpose(
        jnp.sum(head_gradients.astype(jnp.float32) * attn.astype(jnp.float32), axis=-1), (1, 2, 0)
    )
    value_gradient = jnp.einsum(
        "grij,igrd->jgd", probs_b, head_gradients, preferred_element_type=jnp.float32
    )
    dprobs = jnp.einsum(
        "igrd,jgd->grij", head_gradients, heads_of_values, preferred_element_type=jnp.float32
    )
    dscores = (probs * (dprobs - delta[..., None]) * scale).astype(jnp.bfloat16)
    grad_q = jnp.einsum(
        "grij,jgd->igrd", dscores, heads_of_keys, preferred_element_type=jnp.float32
    )
    key_gradient = jnp.einsum(
        "grij,igrd->jgd", dscores, heads_of_queries, preferred_element_type=jnp.float32
    )
    return (
        attn.reshape(rows, -1),
        grad_q.astype(jnp.bfloat16).reshape(rows, -1),
        key_gradient.reshape(length_total, -1),
        value_gradient.reshape(length_total, -1),
    )


def attend(query_rows, keys_in, values_in, grads_in, lengths_all, tiles_all, first_id, second_id):
    seq_ids = jnp.stack([first_id, second_id])
    lengths_pair = jnp.take(lengths_all, seq_ids, axis=0)
    tiles_pair = jnp.take(tiles_all, seq_ids, axis=0)
    ctx_rank = lax.axis_index("ctx")
    seq_dev = query_rows.shape[1]
    keys_all, values_all = (
        lax.all_gather(keys_in, "ctx", axis=1, tiled=True),
        lax.all_gather(values_in, "ctx", axis=1, tiled=True),
    )
    pieces = [
        sequence_core(
            query_rows[seq_slot],
            keys_all[seq_slot],
            values_all[seq_slot],
            grads_in[seq_slot],
            lengths_pair[seq_slot],
            tiles_pair[seq_slot],
            ctx_rank * seq_dev,
        )
        for seq_slot in range(2)
    ]
    attn = jnp.stack([pieces[0][0], pieces[1][0]])
    grad_q = jnp.stack([pieces[0][1], pieces[1][1]])
    key_terms = jnp.stack([pieces[0][2], pieces[1][2]])
    value_terms = jnp.stack([pieces[0][3], pieces[1][3]])
    key_sums, value_sums = (
        lax.psum_scatter(key_terms, "ctx", scatter_dimension=1, tiled=True),
        lax.psum_scatter(value_terms, "ctx", scatter_dimension=1, tiled=True),
    )
    return (attn, grad_q, key_sums.astype(jnp.bfloat16), value_sums.astype(jnp.bfloat16))


def take_second(mine, arrived, swapped):
    return jnp.stack([mine[0], jnp.where(swapped, arrived, mine[1])])


def shards(query_proj, key_proj, value_proj, grad_attn, doc_lengths, mask_tiles, pair_flags):
    dp_size = lax.axis_size("dp")
    dp_rank = lax.axis_index("dp")
    far_bit = dp_size.bit_length() - 2
    partner = jnp.bitwise_xor(dp_rank, dp_size // 2)
    pair_flag = lax.dynamic_index_in_dim(pair_flags, dp_rank, 0, keepdims=False)
    swapped = pair_flag == 1
    first_id = 2 * dp_rank
    second_id = jnp.where(swapped, 2 * partner + 1, 2 * dp_rank + 1)
    arrived = from_partner((query_proj[1], key_proj[1], value_proj[1], grad_attn[1]), "dp", far_bit)
    query_now = take_second(query_proj, arrived[0], swapped)
    key_now = take_second(key_proj, arrived[1], swapped)
    value_now = take_second(value_proj, arrived[2], swapped)
    grad_now = take_second(grad_attn, arrived[3], swapped)
    return attend(
        query_now, key_now, value_now, grad_now, doc_lengths, mask_tiles, first_id, second_id
    )


def solution(mesh):
    in_specs = (
        P("dp", "ctx", None),
        P("dp", "ctx", None),
        P("dp", "ctx", None),
        P("dp", "ctx", None),
        P(),
        P(),
        P(),
    )
    out_specs = (
        P("dp", "ctx", None),
        P("dp", "ctx", None),
        P("dp", "ctx", None),
        P("dp", "ctx", None),
    )
    return jax.shard_map(shards, mesh=mesh, in_specs=in_specs, out_specs=out_specs, check_vma=False)
```

profile of v0, /device:TPU:2, one launch (start us, length us, event | category | flops | bytes accessed | tf_op | source)
XLA Modules:
  0.0 379.0 jit_solution(14901232772893351566)
XLA Ops:
  8.3 1.7 collective-permute-start.1
  11.5 1.2 dynamic_slice.4
  14.0 2.4 collective-permute-done
  18.5 2.2 fusion.67
  20.7 1.6 collective-permute-start.2
  25.7 1.5 gather_fusion.1
  27.2 1.2 reshape_squeeze_stack_squeeze.6
  28.4 1.2 reshape_squeeze_stack_squeeze.7
  31.9 4.0 %collective-permute-done.2 = bf16[64,4096]{1,0:T(8,128)(2,1)} collective-permute-done((bf16[64,4096]{1,0:T(8,128)(2,1)}, bf16[64,4096]{1,0:T(8,128)(2,1)}, u32[]{:S(2)}, u32[]{:S(2)}) %collective-permute-start.2) | collective-permute-done | bytes 524320 | tf_op jit(solution)/shard_map/ppermute | solution.py:14
  35.9 1.1 broadcast_select_fusion.1
  37.0 1.2 reshape_squeeze_stack.6
  38.1 9.8 %collective-permute-done.3 = bf16[64,4096]{1,0:T(8,128)(2,1)} collective-permute-done((bf16[64,4096]{1,0:T(8,128)(2,1)}, bf16[64,4096]{1,0:T(8,128)(2,1)}, u32[]{:S(2)}, u32[]{:S(2)}) %collective-permute-start.3) | collective-permute-done | bytes 524320 | tf_op jit(solution)/shard_map/ppermute | solution.py:14
  48.0 1.1 broadcast_select_fusion
  49.1 1.1 reshape_squeeze_stack.7
  50.2 33.2 %all-gather.3.cloned.1.call-done = bf16[2,512,1024]{2,0,1:T(2,128)(2,1)} async-done(((bf16[2,64,1024]{2,0,1:T(2,128)(2,1)}), bf16[2,512,1024]{2,0,1:T(2,128)(2,1)}) %all-gather.3.cloned.1.call-update) | async-done | bytes 2097168 | tf_op jit(solution)/shard_map/all_gather | solution.py:91
  83.4 6.6 %fusion.65 = (bf16[1,512,1024]{2,0,1:T(2,128)(2,1)}, bf16[1,512,1024]{2,0,1:T(2,128)(2,1)S(1)}) fusion(bf16[2,512,1024]{2,0,1:T(2,128)(2,1)} %all-gather.3.cloned.1.call-done), kind=kLoop, calls=%fused_computation.121 | loop fusion | bytes 4194304 | tf_op jit(solution)/shard_map/slice | solution.py:97
  90.0 5.8 %copy.180 = bf16[1,512,1024]{1,2,0:T(8,128)(2,1)} copy(bf16[1,512,1024]{2,0,1:T(2,128)(2,1)} %get-tuple-element.8) | data formatting | bytes 2097152
  95.8 4.2 %copy.182 = bf16[1,512,1024]{1,2,0:T(8,128)(2,1)} copy(bf16[1,512,1024]{2,0,1:T(2,128)(2,1)S(1)} %get-tuple-element.9) | data formatting | bytes 2097152
  100.0 45.6 %all-gather.5.cloned.1.call-done = bf16[2,512,1024]{2,0,1:T(2,128)(2,1)} async-done(((bf16[2,64,1024]{2,0,1:T(2,128)(2,1)}), bf16[2,512,1024]{2,0,1:T(2,128)(2,1)}) %all-gather.5.cloned.1.call-update) | async-done | bytes 2097168 | tf_op jit(solution)/shard_map/all_gather | solution.py:90
  145.6 6.5 %fusion.64 = (bf16[1,512,1024]{2,0,1:T(2,128)(2,1)S(1)}, bf16[1,512,1024]{2,0,1:T(2,128)(2,1)}) fusion(bf16[2,512,1024]{2,0,1:T(2,128)(2,1)} %all-gather.5.cloned.1.call-done), kind=kLoop, calls=%fused_computation.120 | loop fusion | bytes 4194304 | tf_op jit(solution)/shard_map/slice | solution.py:96
  152.1 2.6 copy.181
  154.7 4.6 %copy.183 = bf16[1,512,1024]{1,2,0:T(8,128)(2,1)S(1)} copy(bf16[1,512,1024]{2,0,1:T(2,128)(2,1)} %get-tuple-element.7) | data formatting | bytes 2097152
  159.2 1.7 fusion.30
  161.0 2.1 fusion.70
  164.6 1.5 multiply_reduce_fusion
  166.1 1.1 fusion.4
  167.3 2.0 fusion.28
  169.3 2.9 copy.147
  172.9 2.1 fusion.71
  176.6 1.5 multiply_reduce_fusion.1
  179.2 2.1 fusion.32
  181.3 2.9 copy.146
  184.1 4.7 %pad_maximum_fusion = f32[2,512,1024]{2,1,0:T(8,128)} fusion(f32[1,512,1024]{2,1,0:T(8,128)} %copy.147, f32[1,512,1024]{2,1,0:T(8,128)} %copy.146), kind=kLoop, calls=%fused_computation.4 | loop fusion | flops 1048576 | bytes 8388608 | tf_op jit(solution)/shard_map/stack | solution.py:107
  189.9 3.5 fusion.36
  193.4 2.9 copy.151
  196.3 3.5 fusion.39
  199.8 3.0 copy.150
  202.8 4.8 %pad_maximum_fusion.1 = f32[2,512,1024]{2,1,0:T(8,128)} fusion(f32[1,512,1024]{2,1,0:T(8,128)} %copy.151, f32[1,512,1024]{2,1,0:T(8,128)} %copy.150), kind=kLoop, calls=%fused_computation.5 | loop fusion | flops 1048576 | bytes 8388608 | tf_op jit(solution)/shard_map/stack | solution.py:108
  207.6 2.3 fusion.21
  209.9 1.2 copy.143
  211.1 2.3 stack_reshape.27
  213.4 2.2 copy.133
  215.6 2.3 stack_reshape.25
  219.4 1.5 copy.127
  223.4 54.4 %reduce-scatter.3.cloned.1.call-done = f32[2,64,1024]{2,1,0:T(8,128)} async-done(((f32[2,512,1024]{2,1,0:T(8,128)}), f32[2,64,1024]{2,1,0:T(8,128)}) %reduce-scatter.3.cloned.1.call-update) | async-done | bytes 524304 | tf_op jit(solution)/shard_map/reduce_scatter | solution.py:110
  277.8 1.8 convert_element_type.106
  279.6 91.1 %reduce-scatter.5.cloned.1.call-done = f32[2,64,1024]{2,1,0:T(8,128)} async-done(((f32[2,512,1024]{2,1,0:T(8,128)}), f32[2,64,1024]{2,1,0:T(8,128)}) %reduce-scatter.5.cloned.1.call-update) | async-done | bytes 524304 | tf_op jit(solution)/shard_map/reduce_scatter | solution.py:111
  370.7 1.8 convert_element_type.107
  (86 shorter events, 20.9 us)
Async XLA Ops:
  7.2 15.1 %copy-start.8 = (bf16[2,64,4096]{2,1,0:T(8,128)(2,1)S(1)}, bf16[2,64,4096]{2,1,0:T(8,128)(2,1)}, u32[]{:S(2)}) copy-start(bf16[2,64,4096]{2,1,0:T(8,128)(2,1)} %param.10) | copy-start | bytes 3145732
  7.2 16.4 %copy-start.17 = (s32[64,8]{0,1:T(8,128)S(1)}, s32[64,8]{0,1:T(8,128)}, u32[]{:S(2)}) copy-start(s32[64,8]{0,1:T(8,128)} %param.11) | copy-start | bytes 6148
  7.2 17.7 %copy-start.16 = (s32[64,8,8]{0,2,1:T(8,128)S(1)}, s32[64,8,8]{0,2,1:T(8,128)}, u32[]{:S(2)}) copy-start(s32[64,8,8]{0,2,1:T(8,128)} %param.12) | copy-start | bytes 49156
  7.2 76.2 %all-gather.3.cloned.1.call-start = ((), (), s32[]{:S(2)}) async-start(), calls=%async_computation.2 | async-start | bytes 2359296 | tf_op jit(solution)/shard_map/all_gather | solution.py:91
  8.3 5.7 %collective-permute-start.1 = (bf16[64,1024]{1,0:T(8,128)(2,1)S(1)}, bf16[64,1024]{1,0:T(8,128)(2,1)S(1)}, u32[]{:S(2)}, u32[]{:S(2)}) collective-permute-start(bf16[64,1024]{1,0:T(8,128)(2,1)S(1)} %get-tuple-element.15), channel_id=1, source_target_pairs={{0,128},{8,136},{16,144},{24,152},{32,160},{40,168},{48,176},{56,1... | collective-permute-start | bytes 393224 | tf_op jit(solution)/shard_map/ppermute | solution.py:14
  11.0 5.5 %collective-permute-start = (bf16[64,1024]{1,0:T(8,128)(2,1)S(1)}, bf16[64,1024]{1,0:T(8,128)(2,1)S(1)}, u32[]{:S(2)}, u32[]{:S(2)}) collective-permute-start(bf16[64,1024]{1,0:T(8,128)(2,1)S(1)} %get-tuple-element.17), channel_id=1, source_target_pairs={{0,128},{8,136},{16,144},{24,152},{32,160},{40,168},{48,176},{56,1... | collective-permute-start | bytes 393224 | tf_op jit(solution)/shard_map/ppermute | solution.py:14
  18.5 17.4 %copy-start.7 = (bf16[2,64,4096]{2,1,0:T(8,128)(2,1)S(1)}, bf16[2,64,4096]{2,1,0:T(8,128)(2,1)}, u32[]{:S(2)}) copy-start(bf16[2,64,4096]{2,1,0:T(8,128)(2,1)} %param.7) | copy-start | bytes 3145732
  18.5 127.1 %all-gather.5.cloned.1.call-start = ((), (), s32[]{:S(2)}) async-start(), calls=%async_computation.3 | async-start | bytes 2359296 | tf_op jit(solution)/shard_map/all_gather | solution.py:90
  20.7 15.2 %collective-permute-start.2 = (bf16[64,4096]{1,0:T(8,128)(2,1)}, bf16[64,4096]{1,0:T(8,128)(2,1)}, u32[]{:S(2)}, u32[]{:S(2)}) collective-permute-start(bf16[64,4096]{1,0:T(8,128)(2,1)} %get-tuple-element.13), channel_id=1, source_target_pairs={{0,128},{8,136},{16,144},{24,152},{32,160},{40,168},{48,176},{56,1... | collective-permute-start | bytes 1572872 | tf_op jit(solution)/shard_map/ppermute | solution.py:14
  23.1 24.8 %collective-permute-start.3 = (bf16[64,4096]{1,0:T(8,128)(2,1)}, bf16[64,4096]{1,0:T(8,128)(2,1)}, u32[]{:S(2)}, u32[]{:S(2)}) collective-permute-start(bf16[64,4096]{1,0:T(8,128)(2,1)} %get-tuple-element.11), channel_id=1, source_target_pairs={{0,128},{8,136},{16,144},{24,152},{32,160},{40,168},{48,176},{56,1... | collective-permute-start | bytes 1572872 | tf_op jit(solution)/shard_map/ppermute | solution.py:14
  30.8 247.1 %reduce-scatter.3.cloned.1.call-start = ((), (), s32[]{:S(2)}) async-start(), calls=%async_computation.4 | async-start | bytes 4718592 | tf_op jit(solution)/shard_map/reduce_scatter | solution.py:110
  163.1 1.0 copy-start.10
  163.1 1.5 copy-start.15
  163.5 3.8 copy-start
  166.1 1.1 copy-start.6
  167.3 2.0 copy-start.2
  167.3 4.9 %copy-start.5 = (bf16[64,8,4,128]{3,2,1,0:T(4,128)(2,1)S(1)}, bf16[64,8,4,128]{3,2,1,0:T(4,128)(2,1)}, u32[]{:S(2)}) copy-start(bf16[64,8,4,128]{3,2,1,0:T(4,128)(2,1)} %reshape_squeeze_stack_squeeze.6) | copy-start | bytes 1572868
  175.0 1.0 copy-start.9
  175.0 1.5 copy-start.14
  175.4 3.8 copy-start.1
  179.2 2.1 copy-start.3
  188.9 1.0 copy-start.11
  188.9 181.8 %reduce-scatter.5.cloned.1.call-start = ((), (), s32[]{:S(2)}) async-start(), calls=%async_computation.5 | async-start | bytes 4718592 | tf_op jit(solution)/shard_map/reduce_scatter | solution.py:111
  209.9 8.0 %copy-start.4 = (bf16[8,4,64,512]{3,2,1,0:T(8,128)(2,1)S(1)}, bf16[8,4,64,512]{3,2,1,0:T(8,128)(2,1)}, u32[]{:S(2)}) copy-start(bf16[8,4,64,512]{3,2,1,0:T(8,128)(2,1)} %copy-done.3) | copy-start | bytes 6291460
  218.6 2.7 copy-start.12
  218.6 3.7 copy-start.13
Sparse Core Ops, SparseCore 0:
  18.6 64.7 all-gather.2
  86.6 58.9 all-gather.4
  189.0 88.7 reduce-scatter.2
  281.9 88.7 reduce-scatter.4
where the time goes:
time: 380 us; the launch traced here: 379 us
  waiting for transfers between devices  241 us (63%)
  local copies, waits for them, and re-layouts  71.7 us (19%)
  other arithmetic  24.4 us (6%)
  matrix products  22.5 us (6%)
  between operations  14.8 us (4%)
  starting transfers between devices  4.39 us (1%)
    reduce_scatter x1, waiting for transfers between devices, attend(): lax.psum_scatter(value_terms, 'ctx', scatter_dimension=1, tiled=True)  91.1 us
    reduce_scatter x1, waiting for transfers between devices, attend(): lax.psum_scatter(key_terms, 'ctx', scatter_dimension=1, tiled=True)  54.4 us
    all_gather x1, waiting for transfers between devices, attend(): lax.all_gather(keys_in, 'ctx', axis=1, tiled=True)  45.6 us
    all_gather x1, waiting for transfers between devices, attend(): lax.all_gather(values_in, 'ctx', axis=1, tiled=True)  33.2 us
    unnamed x42, local copies, waits for them, and re-layouts  21.4 us
    ppermute x4, waiting for transfers between devices, from_partner(): return lax.ppermute(value, axis, pairs)  16.9 us
  transfers between devices with their start and end apart: 8, of which 8 were waited for; matrix products, arithmetic and copies ran while one was open for 18% of the time, Pallas kernels for 0%

commit v1 on v0

--- a/solution.py
+++ b/solution.py
@@ -87,7 +87,15 @@
     ctx_rank = lax.axis_index("ctx")
     seq_dev = query_rows.shape[1]
     keys_all, values_all = (
-        lax.all_gather(keys_in, "ctx", axis=1, tiled=True),
+        jnp.concatenate(
+            lax.all_to_all(
+                jnp.stack([keys_in] * lax.axis_size("ctx")),
+                axis_name="ctx",
+                split_axis=0,
+                concat_axis=0,
+            ),
+            axis=1,
+        ),
         lax.all_gather(values_in, "ctx", axis=1, tiled=True),
     )
     pieces = [

time: 380 us -> 300 us (0.79)
  waiting for transfers between devices: 241 us -> 163 us
  local copies, waits for them, and re-layouts: 71.7 us -> 57 us
  starting transfers between devices: 4.39 us -> 11.9 us
  matrix products: 22.5 us -> 27.8 us
    reduce_scatter x1, waiting for transfers between devices: 91.1 us -> 34.1 us  [attend(): lax.psum_scatter(value_terms, 'ctx', scatter_dimension=1, tiled=True)]
    all_gather x1 -> x0, waiting for transfers between devices: 45.6 us -> none  [attend(): lax.all_gather(keys_in, 'ctx', axis=1, tiled=True)]
    reduce_scatter x1, waiting for transfers between devices: 54.4 us -> 91.2 us  [attend(): lax.psum_scatter(key_terms, 'ctx', scatter_dimension=1, tiled=True)]
    all_to_all x0 -> x1, waiting for transfers between devices: none -> 20.9 us  [attend(): lax.all_to_all(jnp.stack([keys_in] * lax.axis_size('ctx')), axis_name='ct...]
    all_gather x1, waiting for transfers between devices: 33.2 us -> 13.8 us  [attend(): lax.all_gather(values_in, 'ctx', axis=1, tiled=True)]
    ppermute x4, waiting for transfers between devices: 16.9 us -> 2.53 us  [from_partner(): return lax.ppermute(value, axis, pairs)]
    all_to_all x0 -> x1, starting transfers between devices: none -> 7.46 us  [attend(): lax.all_to_all(jnp.stack([keys_in] * lax.axis_size('ctx')), axis_name='ct...]
    slice x1, local copies, waits for them, and re-layouts: 6.49 us -> 0.17 us  [attend(): keys_all[seq_slot]]
  transfers between devices with their start and end apart: 8 -> 8, of which waited for: 8 -> 5; matrix products, arithmetic and copies ran while one was open for 18% -> 34% of each run, Pallas kernels for 0% -> 0%
where the time goes in v1:
time: 300 us; the launch traced here: 299 us
  waiting for transfers between devices  163 us (54%)
  local copies, waits for them, and re-layouts  57 us (19%)
  matrix products  27.8 us (9%)
  other arithmetic  25.4 us (8%)
  between operations  14.8 us (5%)
  starting transfers between devices  11.9 us (4%)
    reduce_scatter x1, waiting for transfers between devices, attend(): lax.psum_scatter(key_terms, 'ctx', scatter_dimension=1, tiled=True)  91.2 us
    reduce_scatter x1, waiting for transfers between devices, attend(): lax.psum_scatter(value_terms, 'ctx', scatter_dimension=1, tiled=True)  34.1 us
    all_to_all x1, waiting for transfers between devices, attend(): lax.all_to_all(jnp.stack([keys_in] * lax.axis_size('ctx')), axis_name='ct...  20.9 us
    unnamed x44, local copies, waits for them, and re-layouts  17.8 us
    all_gather x1, waiting for transfers between devices, attend(): lax.all_gather(values_in, 'ctx', axis=1, tiled=True)  13.8 us
    all_to_all x1, starting transfers between devices, attend(): lax.all_to_all(jnp.stack([keys_in] * lax.axis_size('ctx')), axis_name='ct...  7.46 us
    dot_general x2, matrix products, sequence_core(): jnp.einsum('grij,jgd->igrd', probs_b, heads_of_values, preferred_element_...  7.32 us
    slice x1, local copies, waits for them, and re-layouts, attend(): values_all[seq_slot]  6.83 us
  transfers between devices with their start and end apart: 8, of which 5 were waited for; matrix products, arithmetic and copies ran while one was open for 34% of the time, Pallas kernels for 0%

profile of v1, /device:TPU:2, one launch (start us, length us, event | category | flops | bytes accessed | tf_op | source)
XLA Modules:
  0.0 299.3 jit_solution(4400337638112103070)
XLA Ops:
  8.3 1.7 collective-permute-start.1
  9.9 1.6 fusion.73
  12.0 2.1 fusion.71
  14.1 1.6 collective-permute-start.2
  15.7 2.1 fusion.70
  21.8 1.0 fusion.23
  24.3 1.2 reshape_squeeze_stack_squeeze.7
  26.6 1.6 stack.60
  28.2 7.5 %all-to-all-start = ((bf16[8,2,64,1024]{3,2,1,0:T(8,128)(2,1)}), bf16[8,2,64,1024]{3,2,1,0:T(8,128)(2,1)S(1)}, u32[]{:S(2)}, u32[]{:S(2)}) async-start(bf16[8,2,64,1024]{3,2,1,0:T(8,128)(2,1)} %stack.60), calls=%async_computation | async-start | bytes 4194304 | tf_op jit(solution)/shard_map/all_to_all | solution.py:91
  35.6 1.9 broadcast_select_fusion.1
  37.5 1.4 reshape_squeeze_stack.6
  38.9 2.5 collective-permute-done.3
  41.5 2.1 broadcast_select_fusion
  43.6 2.2 reshape_squeeze_stack.7
  45.7 20.9 %all-to-all-done = bf16[8,2,64,1024]{3,2,1,0:T(8,128)(2,1)S(1)} async-done(((bf16[8,2,64,1024]{3,2,1,0:T(8,128)(2,1)}), bf16[8,2,64,1024]{3,2,1,0:T(8,128)(2,1)S(1)}, u32[]{:S(2)}, u32[]{:S(2)}) %all-to-all-start) | async-done | bytes 2097184 | tf_op jit(solution)/shard_map/all_to_all | solution.py:91
  68.1 2.1 fusion.74
  70.6 1.3 copy-done.1
  71.9 1.9 fusion.40
  73.8 2.9 copy.143
  77.5 2.1 fusion.75
  80.0 1.3 copy-done
  81.3 1.9 fusion.43
  83.2 2.9 copy.142
  86.2 4.7 %pad_maximum_fusion.1 = f32[2,512,1024]{2,1,0:T(8,128)} fusion(f32[1,512,1024]{2,1,0:T(8,128)} %copy.143, f32[1,512,1024]{2,1,0:T(8,128)} %copy.142), kind=kLoop, calls=%fused_computation.5 | loop fusion | flops 1048576 | bytes 8388608 | tf_op jit(solution)/shard_map/stack | solution.py:116
  91.2 13.8 %all-gather.2.cloned.1.call-done = bf16[2,512,1024]{2,0,1:T(2,128)(2,1)} async-done(((bf16[2,64,1024]{2,0,1:T(2,128)(2,1)}), bf16[2,512,1024]{2,0,1:T(2,128)(2,1)}) %all-gather.2.cloned.1.call-update) | async-done | bytes 2097168 | tf_op jit(solution)/shard_map/all_gather | solution.py:99
  105.0 6.8 %fusion.69 = (bf16[1,512,1024]{2,0,1:T(2,128)(2,1)}, bf16[1,512,1024]{2,0,1:T(2,128)(2,1)}) fusion(bf16[2,512,1024]{2,0,1:T(2,128)(2,1)} %all-gather.2.cloned.1.call-done), kind=kLoop, calls=%fused_computation.125 | loop fusion | bytes 4194304 | tf_op jit(solution)/shard_map/slice | solution.py:105
  111.8 5.8 %copy.172 = bf16[1,512,1024]{1,2,0:T(8,128)(2,1)} copy(bf16[1,512,1024]{2,0,1:T(2,128)(2,1)} %get-tuple-element.8) | data formatting | bytes 2097152
  117.7 5.8 %copy.173 = bf16[1,512,1024]{1,2,0:T(8,128)(2,1)} copy(bf16[1,512,1024]{2,0,1:T(2,128)(2,1)} %get-tuple-element.9) | data formatting | bytes 2097152
  123.5 3.6 %multiply_reduce_fusion = (f32[64,8,4]{0,2,1:T(4,128)S(1)}, bf16[64,8,4,128]{3,0,2,1:T(8,128)(2,1)}) fusion(bf16[64,8,4,128]{3,2,1,0:T(4,128)(2,1)} %reshape_squeeze_stack.7, bf16[512,8,128,1]{0,2,3,1:T(8,128)(2,1)} %bitcast.169, bf16[8,4,64,512]{3,2,1,0:T(8,128)(2,1)} %copy-done.1), kind=kOutput, calls=%fused_computation.46 | convolution fusion | flops 269744128 | bytes 4202496 | tf_op jit(solution)/shard_map/grij,jgd->igrd/dot_general | solution.py:56
  127.2 2.3 fusion.4
  129.5 1.3 copy-done.2
  130.8 1.9 fusion.34
  132.8 3.0 copy.139
  135.7 3.7 %multiply_reduce_fusion.1 = (f32[64,8,4]{0,2,1:T(4,128)S(1)}, bf16[64,8,4,128]{3,0,2,1:T(8,128)(2,1)}) fusion(bf16[64,8,4,128]{3,2,1,0:T(4,128)(2,1)S(1)} %copy-done.9, bf16[512,8,128,1]{0,2,3,1:T(8,128)(2,1)} %bitcast.167, bf16[8,4,64,512]{3,2,1,0:T(8,128)(2,1)} %copy-done), kind=kOutput, calls=%fused_computation.47 | convolution fusion | flops 269744128 | bytes 4202496 | tf_op jit(solution)/shard_map/grij,jgd->igrd/dot_general | solution.py:56
  139.4 2.3 fusion.7
  141.7 1.3 copy-done.3
  143.0 1.9 fusion.37
  144.9 2.9 copy.138
  147.8 4.9 %pad_maximum_fusion = f32[2,512,1024]{2,1,0:T(8,128)} fusion(f32[1,512,1024]{2,1,0:T(8,128)} %copy.139, f32[1,512,1024]{2,1,0:T(8,128)} %copy.138), kind=kLoop, calls=%fused_computation.4 | loop fusion | flops 1048576 | bytes 8388608 | tf_op jit(solution)/shard_map/stack | solution.py:115
  152.8 2.4 fusion.21
  156.8 2.3 fusion.20
  159.9 1.5 copy.120
  161.8 1.1 pad_maximum_fusion.3
  162.9 1.1 pad_maximum_fusion.2
  163.9 34.1 %reduce-scatter.5.cloned.1.call-done = f32[2,64,1024]{2,1,0:T(8,128)} async-done(((f32[2,512,1024]{2,1,0:T(8,128)}), f32[2,64,1024]{2,1,0:T(8,128)}) %reduce-scatter.5.cloned.1.call-update) | async-done | bytes 524304 | tf_op jit(solution)/shard_map/reduce_scatter | solution.py:119
  198.0 1.8 convert_element_type.107
  199.8 91.2 %reduce-scatter.3.cloned.1.call-done = f32[2,64,1024]{2,1,0:T(8,128)} async-done(((f32[2,512,1024]{2,1,0:T(8,128)}), f32[2,64,1024]{2,1,0:T(8,128)}) %reduce-scatter.3.cloned.1.call-update) | async-done | bytes 524304 | tf_op jit(solution)/shard_map/reduce_scatter | solution.py:118
  291.0 1.8 convert_element_type.106
  (87 shorter events, 13.3 us)
Async XLA Ops:
  7.2 11.1 %copy-start.16 = (s32[32]{0:T(128)S(1)}, s32[32]{0:T(128)}, u32[]{:S(2)}) copy-start(s32[32]{0:T(128)} %param.13) | copy-start | bytes 388
  7.2 12.4 %copy-start.15 = (s32[64,8]{0,1:T(8,128)S(1)}, s32[64,8]{0,1:T(8,128)}, u32[]{:S(2)}) copy-start(s32[64,8]{0,1:T(8,128)} %param.11) | copy-start | bytes 6148
  7.2 13.8 %copy-start.14 = (s32[64,8,8]{0,2,1:T(8,128)S(1)}, s32[64,8,8]{0,2,1:T(8,128)}, u32[]{:S(2)}) copy-start(s32[64,8,8]{0,2,1:T(8,128)} %param.12) | copy-start | bytes 49156
  7.2 97.8 %all-gather.2.cloned.1.call-start = ((), (), s32[]{:S(2)}) async-start(), calls=%async_computation.3 | async-start | bytes 2359296 | tf_op jit(solution)/shard_map/all_gather | solution.py:99
  8.2 17.2 %copy-start.11 = (bf16[2,64,1024]{2,1,0:T(8,128)(2,1)S(1)}, bf16[2,64,1024]{2,1,0:T(8,128)(2,1)}, u32[]{:S(2)}) copy-start(bf16[2,64,1024]{2,1,0:T(8,128)(2,1)} %param.8) | copy-start | bytes 786436
  8.2 17.2 %copy-start.12 = (bf16[2,64,1024]{2,1,0:T(8,128)(2,1)S(1)}, bf16[2,64,1024]{2,1,0:T(8,128)(2,1)}, u32[]{:S(2)}) copy-start(bf16[2,64,1024]{2,1,0:T(8,128)(2,1)} %param.9) | copy-start | bytes 786436
  8.3 17.2 %collective-permute-start.1 = (bf16[64,1024]{1,0:T(8,128)(2,1)S(1)}, bf16[64,1024]{1,0:T(8,128)(2,1)S(1)}, u32[]{:S(2)}, u32[]{:S(2)}) collective-permute-start(bf16[64,1024]{1,0:T(8,128)(2,1)S(1)} %get-tuple-element.15), channel_id=1, source_target_pairs={{0,128},{8,136},{16,144},{24,152},{32,160},{40,168},{48,176},{56,1... | collective-permute-start | bytes 393224 | tf_op jit(solution)/shard_map/ppermute | solution.py:14
  11.6 13.9 %collective-permute-start = (bf16[64,1024]{1,0:T(8,128)(2,1)}, bf16[64,1024]{1,0:T(8,128)(2,1)S(1)}, u32[]{:S(2)}, u32[]{:S(2)}) collective-permute-start(bf16[64,1024]{1,0:T(8,128)(2,1)} %get-tuple-element.17), channel_id=1, source_target_pairs={{0,128},{8,136},{16,144},{24,152},{32,160},{40,168},{48,176},{56,1... | collective-permute-start | bytes 393224 | tf_op jit(solution)/shard_map/ppermute | solution.py:14
  14.1 21.5 %collective-permute-start.2 = (bf16[64,4096]{1,0:T(8,128)(2,1)}, bf16[64,4096]{1,0:T(8,128)(2,1)S(1)}, u32[]{:S(2)}, u32[]{:S(2)}) collective-permute-start(bf16[64,4096]{1,0:T(8,128)(2,1)} %get-tuple-element.13), channel_id=1, source_target_pairs={{0,128},{8,136},{16,144},{24,152},{32,160},{40,168},{48,176},{56,1... | collective-permute-start | bytes 1572872 | tf_op jit(solution)/shard_map/ppermute | solution.py:14
  17.8 23.7 %collective-permute-start.3 = (bf16[64,4096]{1,0:T(8,128)(2,1)}, bf16[64,4096]{1,0:T(8,128)(2,1)}, u32[]{:S(2)}, u32[]{:S(2)}) collective-permute-start(bf16[64,4096]{1,0:T(8,128)(2,1)} %get-tuple-element.11), channel_id=1, source_target_pairs={{0,128},{8,136},{16,144},{24,152},{32,160},{40,168},{48,176},{56,1... | collective-permute-start | bytes 1572872 | tf_op jit(solution)/shard_map/ppermute | solution.py:14
  28.2 38.4 %all-to-all-start = ((bf16[8,2,64,1024]{3,2,1,0:T(8,128)(2,1)}), bf16[8,2,64,1024]{3,2,1,0:T(8,128)(2,1)S(1)}, u32[]{:S(2)}, u32[]{:S(2)}) async-start(bf16[8,2,64,1024]{3,2,1,0:T(8,128)(2,1)} %stack.60), calls=%async_computation | async-start | bytes 4194304 | tf_op jit(solution)/shard_map/all_to_all | solution.py:91
  35.6 162.4 %reduce-scatter.5.cloned.1.call-start = ((), (), s32[]{:S(2)}) async-start(), calls=%async_computation.5 | async-start | bytes 4718592 | tf_op jit(solution)/shard_map/reduce_scatter | solution.py:119
  67.0 1.0 copy-start.18
  70.2 3.6 %copy-start.6 = (f32[8,4,64,512]{3,2,1,0:T(8,128)}, f32[8,4,64,512]{3,2,1,0:T(8,128)S(1)}, u32[]{:S(2)}) copy-start(f32[8,4,64,512]{3,2,1,0:T(8,128)S(1)} %get-tuple-element.21) | copy-start | bytes 12582916
  70.2 1.7 copy-start.10
  70.6 1.3 copy-start.1
  73.8 3.6 %copy-start.17 = (pred[64,512]{1,0:T(8,128)(4,1)S(1)}, pred[64,512]{1,0:T(8,128)(4,1)}, u32[]{:S(2)}) copy-start(pred[64,512]{1,0:T(8,128)(4,1)} %fusion.22) | copy-start | bytes 98308
  79.6 3.6 %copy-start.4 = (f32[8,4,64,512]{3,2,1,0:T(8,128)}, f32[8,4,64,512]{3,2,1,0:T(8,128)S(1)}, u32[]{:S(2)}) copy-start(f32[8,4,64,512]{3,2,1,0:T(8,128)S(1)} %get-tuple-element.23) | copy-start | bytes 12582916
  79.6 1.7 copy-start.8
  80.0 1.3 copy-start
  90.9 200.0 %reduce-scatter.3.cloned.1.call-start = ((), (), s32[]{:S(2)}) async-start(), calls=%async_computation.4 | async-start | bytes 4718592 | tf_op jit(solution)/shard_map/reduce_scatter | solution.py:118
  123.5 3.7 %copy-start.7 = (f32[8,4,64,512]{3,2,1,0:T(8,128)S(1)}, f32[8,4,64,512]{3,2,1,0:T(8,128)}, u32[]{:S(2)}) copy-start(f32[8,4,64,512]{3,2,1,0:T(8,128)} %copy-done.6) | copy-start | bytes 12582916
  129.5 1.4 copy-start.2
  132.8 3.0 copy-start.9
  135.7 3.7 %copy-start.5 = (f32[8,4,64,512]{3,2,1,0:T(8,128)S(1)}, f32[8,4,64,512]{3,2,1,0:T(8,128)}, u32[]{:S(2)}) copy-start(f32[8,4,64,512]{3,2,1,0:T(8,128)} %copy-done.4) | copy-start | bytes 12582916
  141.7 1.3 copy-start.3
  152.8 3.2 %copy-start.13 = (bf16[64,8,4,128]{3,0,2,1:T(8,128)(2,1)S(1)}, bf16[64,8,4,128]{3,0,2,1:T(8,128)(2,1)}, u32[]{:S(2)}) copy-start(bf16[64,8,4,128]{3,0,2,1:T(8,128)(2,1)} %get-tuple-element.25) | copy-start | bytes 1572868
Sparse Core Ops, SparseCore 0:
  26.6 78.3 all-gather.1
  109.2 88.7 reduce-scatter.4
  202.2 88.7 reduce-scatter.2
